TPU v7x, 256 devices: a whole 4x4x8 slice. The times are simulated.
256 devices in a mesh: expert: 16 (over y, x), hidden: 16 (over z, core).
Axes of the slice: x: 4, y: 4, z: 8, core: 2. Of those that a mesh axis runs over, the one named last changes fastest.
Arguments:
- layer_input: bfloat16 [4096, 4096], P('expert', 'hidden'), may hold values from -6 to 6
- output_grad: bfloat16 [4096, 4096], P('expert', 'hidden'), may hold values from -1.5 to 1.5
- latent_saved: bfloat16 [4096, 1024], P('expert'), may hold values from -6 to 6
- combined_saved: bfloat16 [4096, 1024], P('expert'), may hold values from -6 to 6
- expert_ids: int32 [4096, 22], P('expert'), may hold values from 0 to 511, as said below
- gate_values: bfloat16 [4096, 22], P('expert'), may hold values from 0.099609375 to 1.5
- down_proj: bfloat16 [1024, 4096], P(None, 'hidden'), may hold values from -0.09375 to 0.09375
- up_proj: bfloat16 [1024, 4096], P(None, 'hidden'), may hold values from -0.1875 to 0.1875
- expert_in: bfloat16 [16, 1024, 2688], P('expert', None, 'hidden'), may hold values from -0.1875 to 0.1875
- expert_out: bfloat16 [16, 2688, 1024], P('expert', 'hidden'), may hold values from -0.125 to 0.125
Outputs:
- input_grad: bfloat16 [4096, 4096], P('expert', 'hidden')
- down_grad: float32 [1024, 4096], P('expert', 'hidden')
- up_grad: float32 [1024, 4096], P('expert', 'hidden')
- gate_grad: float32 [4096, 22], P('expert')
- expert_in_grad: float32 [16, 1024, 2688], P('expert', None, 'hidden')
- expert_out_grad: float32 [16, 2688, 1024], P('expert', 'hidden')
Inputs may be any that keep to these rules, and one draw needn't show every extreme that they name: `expert_ids`: each row names 22 different experts. In each aligned block of 256 rows (the rows of one index of the expert axis) each expert below 16 is named by at most 24 rows; some expert below 16 is named by exactly 24 rows in every block.
All inputs are finite; a program needn't handle non-finite values.
Results may differ from a plain program's by a relative error of at most 0.0065.
Values may be sent and summed in bfloat16 or wider, within the bound.
No kernel may reach another device: no remote copies, remote signals or barrier semaphores. Data moves between devices by JAX's collectives and lax.ppermute only.
A program may use at most 64 MiB of HBM per device.

v0:
```python
import jax
import jax.numpy as jnp
from jax import lax
from jax.sharding import PartitionSpec as P


def slot_layout(table, groups, local_count):
    tokens_here = table.shape[0]
    return table.T.reshape(groups, local_count, tokens_here).transpose(1, 0, 2)[:, :, None, :]


def on_device(
    layer_input,
    output_grad,
    latent_saved,
    combined_saved,
    expert_ids,
    gate_values,
    down_proj,
    up_proj,
    expert_in,
    expert_out,
):
    groups = lax.axis_size("expert")
    tokens_here = layer_input.shape[0]
    latent_width = latent_saved.shape[1]
    local_count = expert_in.shape[0]
    capacity = tokens_here * 3 // 32
    live_count = local_count * groups
    slot_total = local_count * groups * capacity
    partial_cot = jnp.einsum("td,ld->tl", output_grad, up_proj, preferred_element_type=jnp.float32)
    member = expert_ids[:, :, None] == jnp.arange(live_count, dtype=jnp.int32)[None, None, :]
    per_token = jnp.sum(member.astype(jnp.int32), axis=1)
    before = jnp.cumsum(per_token, axis=0) - per_token
    gate_token = jnp.sum(
        jnp.where(member, gate_values.astype(jnp.float32)[:, :, None], 0.0), axis=1
    )
    rank_iota = jnp.arange(capacity, dtype=jnp.int32)[None, None, :, None]
    hit_slot = (slot_layout(per_token, groups, local_count) == 1) & (
        slot_layout(before, groups, local_count) == rank_iota
    )
    gate_slot = jnp.sum(
        jnp.where(hit_slot, slot_layout(gate_token, groups, local_count), 0.0), axis=3
    )
    gate_send = gate_slot.astype(jnp.bfloat16)
    dispatch_bf = hit_slot.astype(jnp.bfloat16).reshape(slot_total, tokens_here)
    cot_full = lax.psum(partial_cot, "hidden")
    cot_rows = jnp.dot(
        dispatch_bf, cot_full.astype(jnp.bfloat16), preferred_element_type=jnp.float32
    ).astype(jnp.bfloat16)
    latent_rows = jnp.dot(dispatch_bf, latent_saved, preferred_element_type=jnp.float32).astype(
        jnp.bfloat16
    )
    cot_recv, latent_recv, gate_recv = (
        lax.all_to_all(
            cot_rows.reshape(local_count, groups, capacity, latent_width),
            "expert",
            split_axis=1,
            concat_axis=1,
            tiled=True,
        ),
        lax.all_to_all(
            latent_rows.reshape(local_count, groups, capacity, latent_width),
            "expert",
            split_axis=1,
            concat_axis=1,
            tiled=True,
        ),
        lax.all_to_all(gate_send, "expert", split_axis=1, concat_axis=1, tiled=True),
    )
    row_count = groups * capacity
    cot_block = cot_recv.reshape(local_count, row_count, latent_width)
    latent_block = latent_recv.reshape(local_count, row_count, latent_width)
    gate_block = gate_recv.reshape(local_count, row_count).astype(jnp.float32)
    pre_act = jnp.einsum(
        "erl,elf->erf", latent_block, expert_in, preferred_element_type=jnp.float32
    )
    relu_out = jnp.maximum(pre_act, 0.0)
    back_proj = jnp.einsum(
        "erl,efl->erf", cot_block, expert_out, preferred_element_type=jnp.float32
    )
    gate_part = jnp.sum(back_proj * relu_out * relu_out, axis=2)
    scaled_act = (gate_block[:, :, None] * relu_out * relu_out).astype(jnp.bfloat16)
    pre_grad = (2.0 * gate_block[:, :, None] * relu_out * back_proj).astype(jnp.bfloat16)
    expert_out_grad = jnp.einsum(
        "erf,erl->efl", scaled_act, cot_block, preferred_element_type=jnp.float32
    )
    expert_in_grad = jnp.einsum(
        "erl,erf->elf", latent_block, pre_grad, preferred_element_type=jnp.float32
    )
    latent_back = jnp.einsum(
        "erf,elf->erl", pre_grad, expert_in, preferred_element_type=jnp.float32
    )
    latent_back = latent_back.reshape(local_count, groups, capacity, latent_width)
    gate_part = gate_part.reshape(local_count, groups, capacity)
    dispatch_full = hit_slot.astype(jnp.float32)
    dispatch_flat = dispatch_full.reshape(slot_total, tokens_here)
    rows_home, gate_home = (
        lax.all_to_all(latent_back, "expert", split_axis=1, concat_axis=1, tiled=True),
        lax.all_to_all(gate_part, "expert", split_axis=1, concat_axis=1, tiled=True),
    )
    token_sums = jnp.dot(
        dispatch_flat.T,
        rows_home.reshape(slot_total, latent_width),
        precision=lax.Precision.HIGHEST,
        preferred_element_type=jnp.float32,
    )
    by_expert = jnp.sum(dispatch_full * gate_home[:, :, :, None], axis=2)
    by_expert = by_expert.transpose(2, 1, 0).reshape(tokens_here, live_count)
    gate_local = jnp.sum(jnp.where(member, by_expert[:, None, :], 0.0), axis=2)
    latent_grad, gate_grad = lax.psum((token_sums, gate_local), "hidden")
    latent_bf = latent_grad.astype(jnp.bfloat16)
    input_grad = jnp.dot(latent_bf, down_proj, preferred_element_type=jnp.float32).astype(
        jnp.bfloat16
    )
    down_term = jnp.einsum("tl,td->ld", latent_bf, layer_input, preferred_element_type=jnp.float32)
    up_term = jnp.einsum(
        "tl,td->ld", combined_saved, output_grad, preferred_element_type=jnp.float32
    )
    down_grad, up_grad = (
        lax.psum_scatter(down_term, "expert", scatter_dimension=0, tiled=True),
        lax.psum_scatter(up_term, "expert", scatter_dimension=0, tiled=True),
    )
    return (input_grad, down_grad, up_grad, gate_grad, expert_in_grad, expert_out_grad)


def solution(mesh):
    return jax.shard_map(
        on_device,
        mesh=mesh,
        in_specs=(
            P("expert", "hidden"),
            P("expert", "hidden"),
            P("expert", None),
            P("expert", None),
            P("expert", None),
            P("expert", None),
            P(None, "hidden"),
            P(None, "hidden"),
            P("expert", None, "hidden"),
            P("expert", "hidden", None),
        ),
        out_specs=(
            P("expert", "hidden"),
            P("expert", "hidden"),
            P("expert", "hidden"),
            P("expert", None),
            P("expert", None, "hidden"),
            P("expert", "hidden", None),
        ),
        check_vma=False,
    )
```

profile of v0, /device:TPU:2, one launch (start us, length us, event | category | flops | bytes accessed | tf_op | source)
XLA Modules:
  0.0 312.9 jit_solution(7600036610667485425)
XLA Ops:
  7.2 0.8 convert_reduce_fusion
  9.0 1.5 fusion.23
  10.5 62.0 %all-reduce.3 = bf16[256,1024]{1,0:T(8,128)(2,1)S(1)} all-reduce(f32[256,1024]{1,0:T(8,128)S(1)} %fusion.23), channel_id=1, replica_groups=mesh['expert'=16,'hidden'=16] {'hidden'}, use_global_device_ids=true, to_apply=%region_5.6 | all-reduce | flops 262144 | bytes 1572864 | tf_op jit(solution)/shard_map/psum | solution.py:47
  72.7 1.3 convolution_convert_fusion
  73.9 7.5 %all-to-all-start.2 = ((bf16[1,16,24,1024]{3,2,0,1:T(8,128)(2,1)}), bf16[1,16,24,1024]{3,2,0,1:T(8,128)(2,1)S(1)}, u32[]{:S(2)}, u32[]{:S(2)}) async-start(bf16[1,16,24,1024]{3,2,0,1:T(8,128)(2,1)} %bitcast.11), calls=%async_computation.2 | async-start | bytes 1572864 | tf_op jit(solution)/shard_map/all_to_all | solution.py:55
  81.4 1.3 convolution_convert_fusion.1
  82.7 8.9 %all-to-all-done.2 = bf16[1,16,24,1024]{3,2,0,1:T(8,128)(2,1)S(1)} async-done(((bf16[1,16,24,1024]{3,2,0,1:T(8,128)(2,1)}), bf16[1,16,24,1024]{3,2,0,1:T(8,128)(2,1)S(1)}, u32[]{:S(2)}, u32[]{:S(2)}) %all-to-all-start.2) | async-done | bytes 786464 | tf_op jit(solution)/shard_map/all_to_all | solution.py:55
  91.6 4.9 %all-to-all-start.1 = ((bf16[1,16,24,1024]{3,2,0,1:T(8,128)(2,1)}), bf16[1,16,24,1024]{3,2,0,1:T(8,128)(2,1)S(1)}, u32[]{:S(2)}, u32[]{:S(2)}) async-start(bf16[1,16,24,1024]{3,2,0,1:T(8,128)(2,1)} %bitcast.7), calls=%async_computation.1 | async-start | bytes 1572864 | tf_op jit(solution)/shard_map/all_to_all | solution.py:62
  96.9 9.9 %all-to-all-done.1 = bf16[1,16,24,1024]{3,2,0,1:T(8,128)(2,1)S(1)} async-done(((bf16[1,16,24,1024]{3,2,0,1:T(8,128)(2,1)}), bf16[1,16,24,1024]{3,2,0,1:T(8,128)(2,1)S(1)}, u32[]{:S(2)}, u32[]{:S(2)}) %all-to-all-start.1) | async-done | bytes 786464 | tf_op jit(solution)/shard_map/all_to_all | solution.py:62
  107.2 0.7 reshape.184
  107.9 4.7 %all-to-all-start.4 = ((f32[1,16,24]{2,0,1:T(1,128)}), f32[1,16,24]{2,0,1:T(1,128)S(1)}, u32[]{:S(2)}, u32[]{:S(2)}) async-start(f32[1,16,24]{2,0,1:T(1,128)} %reshape.184), calls=%async_computation.6 | async-start | bytes 16384 | tf_op jit(solution)/shard_map/all_to_all | solution.py:100
  112.7 6.2 %all-to-all-done.4 = f32[1,16,24]{2,0,1:T(1,128)S(1)} async-done(((f32[1,16,24]{2,0,1:T(1,128)}), f32[1,16,24]{2,0,1:T(1,128)S(1)}, u32[]{:S(2)}, u32[]{:S(2)}) %all-to-all-start.4) | async-done | bytes 1568 | tf_op jit(solution)/shard_map/all_to_all | solution.py:100
  119.4 10.6 %all_to_all.25 = bf16[1,16,24]{2,0,1:T(2,128)(2,1)S(1)} all-to-all(bf16[1,16,24]{2,0,1:T(2,128)(2,1)S(1)} %copy.45), channel_id=1, replica_groups=mesh['expert'=16,'hidden'=16] {'expert'}, dimensions={1} | all-to-all | bytes 1536 | tf_op jit(solution)/shard_map/all_to_all | solution.py:69
  130.3 1.5 convolution_bitcast_fusion
  131.8 5.7 %all-to-all-start.3 = ((f32[1,16,24,1024]{3,2,0,1:T(8,128)}), f32[1,16,24,1024]{3,2,0,1:T(8,128)}, u32[]{:S(2)}, u32[]{:S(2)}) async-start(f32[1,16,24,1024]{3,2,0,1:T(8,128)} %convolution_bitcast_fusion), calls=%async_computation.3 | async-start | bytes 3145728 | tf_op jit(solution)/shard_map/all_to_all | solution.py:99
  137.6 1.3 fusion.24
  139.0 13.1 %all-to-all-done.3 = f32[1,16,24,1024]{3,2,0,1:T(8,128)} async-done(((f32[1,16,24,1024]{3,2,0,1:T(8,128)}), f32[1,16,24,1024]{3,2,0,1:T(8,128)}, u32[]{:S(2)}, u32[]{:S(2)}) %all-to-all-start.3) | async-done | bytes 1572896 | tf_op jit(solution)/shard_map/all_to_all | solution.py:99
  152.1 3.5 %fusion.2 = f32[256,1024]{1,0:T(8,128)} fusion(f32[1,16,24,1024]{3,2,0,1:T(8,128)} %all-to-all-done.3, s32[16,256]{1,0:T(8,128)S(1)} %bitcast_subtract_fusion, pred[16,256]{1,0:T(8,128)(4,1)S(1)} %bitcast_compare_fusion.1), kind=kOutput, calls=%fused_computation.5 | convolution fusion | flops 1208156160 | bytes 2641920 | tf_op jit(solution)/shard_map/dot_general | solution.py:102
  155.7 66.5 %all-reduce.4 = (bf16[256,1024]{1,0:T(8,128)(2,1)S(1)}, f32[256,22]{0,1:T(8,128)}) all-reduce(f32[256,1024]{1,0:T(8,128)} %fusion.2, f32[256,22]{0,1:T(8,128)S(1)} %get-tuple-element.6), channel_id=1, replica_groups=mesh['expert'=16,'hidden'=16] {'hidden'}, use_global_device_ids=true, to_apply=%region_6.7 | all-reduce | flops 267776 | bytes 1617920 | tf_op jit(solution)/shard_map/psum | solution.py:111
  222.1 1.3 fusion.25
  223.5 1.2 convolution_bitcast_fusion.2
  224.7 1.2 convolution_bitcast_fusion.1
  225.9 1.0 convolution_convert_fusion.2
  226.9 79.2 %reduce-scatter.3.cloned.1.call-done = f32[64,256]{1,0:T(8,128)} async-done(((f32[1024,256]{1,0:T(8,128)}), f32[64,256]{1,0:T(8,128)}) %reduce-scatter.3.cloned.1.call-update) | async-done | bytes 65552 | tf_op jit(solution)/shard_map/reduce_scatter | solution.py:121
  (45 shorter events, 2.9 us)
Async XLA Ops:
  7.2 74.3 %copy-start = (bf16[256,1024]{1,0:T(8,128)(2,1)S(1)}, bf16[256,1024]{1,0:T(8,128)(2,1)}, u32[]{:S(2)}) copy-start(bf16[256,1024]{1,0:T(8,128)(2,1)} %param.12) | copy-start | bytes 1572868
  73.9 17.7 %all-to-all-start.2 = ((bf16[1,16,24,1024]{3,2,0,1:T(8,128)(2,1)}), bf16[1,16,24,1024]{3,2,0,1:T(8,128)(2,1)S(1)}, u32[]{:S(2)}, u32[]{:S(2)}) async-start(bf16[1,16,24,1024]{3,2,0,1:T(8,128)(2,1)} %bitcast.11), calls=%async_computation.2 | async-start | bytes 1572864 | tf_op jit(solution)/shard_map/all_to_all | solution.py:55
  81.4 15.1 %copy-start.5 = (bf16[1,168,1024]{2,1,0:T(8,128)(2,1)S(1)}, bf16[1,168,1024]{2,1,0:T(8,128)(2,1)}, u32[]{:S(2)}) copy-start(bf16[1,168,1024]{2,1,0:T(8,128)(2,1)} %param.19) | copy-start | bytes 1032196
  82.7 24.0 %copy-start.1 = (bf16[1,1024,168]{1,2,0:T(8,128)(2,1)S(1)}, bf16[1,1024,168]{1,2,0:T(8,128)(2,1)}, u32[]{:S(2)}) copy-start(bf16[1,1024,168]{1,2,0:T(8,128)(2,1)} %param.18) | copy-start | bytes 1032196
  91.6 15.2 %all-to-all-start.1 = ((bf16[1,16,24,1024]{3,2,0,1:T(8,128)(2,1)}), bf16[1,16,24,1024]{3,2,0,1:T(8,128)(2,1)S(1)}, u32[]{:S(2)}, u32[]{:S(2)}) async-start(bf16[1,16,24,1024]{3,2,0,1:T(8,128)(2,1)} %bitcast.7), calls=%async_computation.1 | async-start | bytes 1572864 | tf_op jit(solution)/shard_map/all_to_all | solution.py:62
  96.5 16.2 %copy-start.8 = (bf16[256,22]{0,1:T(8,128)(2,1)S(1)}, bf16[256,22]{0,1:T(8,128)(2,1)}, u32[]{:S(2)}) copy-start(bf16[256,22]{0,1:T(8,128)(2,1)} %param.15) | copy-start | bytes 33796
  96.5 22.5 %copy-start.7 = (s32[256,22]{0,1:T(8,128)S(1)}, s32[256,22]{0,1:T(8,128)}, u32[]{:S(2)}) copy-start(s32[256,22]{0,1:T(8,128)} %param.14) | copy-start | bytes 67588
  107.9 10.9 %all-to-all-start.4 = ((f32[1,16,24]{2,0,1:T(1,128)}), f32[1,16,24]{2,0,1:T(1,128)S(1)}, u32[]{:S(2)}, u32[]{:S(2)}) async-start(f32[1,16,24]{2,0,1:T(1,128)} %reshape.184), calls=%async_computation.6 | async-start | bytes 16384 | tf_op jit(solution)/shard_map/all_to_all | solution.py:100
  131.8 5.8 %copy-start.2 = (bf16[256,1024]{1,0:T(8,128)(2,1)S(1)}, bf16[256,1024]{1,0:T(8,128)(2,1)}, u32[]{:S(2)}) copy-start(bf16[256,1024]{1,0:T(8,128)(2,1)} %param.13) | copy-start | bytes 1572868
  131.8 5.8 %copy-start.4 = (bf16[256,256]{1,0:T(8,128)(2,1)S(1)}, bf16[256,256]{1,0:T(8,128)(2,1)}, u32[]{:S(2)}) copy-start(bf16[256,256]{1,0:T(8,128)(2,1)} %param.11) | copy-start | bytes 393220
  131.8 20.3 %all-to-all-start.3 = ((f32[1,16,24,1024]{3,2,0,1:T(8,128)}), f32[1,16,24,1024]{3,2,0,1:T(8,128)}, u32[]{:S(2)}, u32[]{:S(2)}) async-start(f32[1,16,24,1024]{3,2,0,1:T(8,128)} %convolution_bitcast_fusion), calls=%async_computation.3 | async-start | bytes 3145728 | tf_op jit(solution)/shard_map/all_to_all | solution.py:99
  137.5 89.4 %reduce-scatter.5.cloned.1.call-start = ((), (), s32[]{:S(2)}) async-start(), calls=%async_computation.8 | async-start | bytes 1114112 | tf_op jit(solution)/shard_map/reduce_scatter | solution.py:122
  138.9 83.2 %copy-start.6 = (bf16[256,256]{1,0:T(8,128)(2,1)S(1)}, bf16[256,256]{1,0:T(8,128)(2,1)}, u32[]{:S(2)}) copy-start(bf16[256,256]{1,0:T(8,128)(2,1)} %param.10) | copy-start | bytes 393220
  138.9 167.1 %reduce-scatter.3.cloned.1.call-start = ((), (), s32[]{:S(2)}) async-start(), calls=%async_computation.7 | async-start | bytes 1114112 | tf_op jit(solution)/shard_map/reduce_scatter | solution.py:121
  223.5 2.4 copy-start.3
Sparse Core Ops, SparseCore 0:
  142.4 81.0 reduce-scatter.4
  227.6 78.4 reduce-scatter.2
where the time goes:
time: 313 us
  blocking collectives  139 us (44%)
  waiting for transfers between devices  117 us (37%)
  starting transfers between devices  22.9 us (7%)
  matrix products  15.9 us (5%)
  between operations  14.3 us (5%)
    reduce_scatter x1, waiting for transfers between devices, on_device(): lax.psum_scatter(down_term, 'expert', scatter_dimension=0, tiled=True)  79.2 us
    psum x1, blocking collectives, on_device(): latent_grad, gate_grad = lax.psum((token_sums, gate_local), 'hidden')  66.5 us
    psum x1, blocking collectives, on_device(): cot_full = lax.psum(partial_cot, 'hidden')  62 us
    all_to_all x1, waiting for transfers between devices, on_device(): lax.all_to_all(latent_back, 'expert', split_axis=1, concat_axis=1, tiled=...  13.1 us
    all_to_all x1, blocking collectives, on_device(): lax.all_to_all(gate_send, 'expert', split_axis=1, concat_axis=1, tiled=True)  10.6 us
    all_to_all x1, waiting for transfers between devices, on_device(): lax.all_to_all(latent_rows.reshape(local_count, groups, capacity, latent_...  9.86 us
    all_to_all x1, waiting for transfers between devices, on_device(): lax.all_to_all(cot_rows.reshape(local_count, groups, capacity, latent_wid...  8.87 us
    all_to_all x1, starting transfers between devices, on_device(): lax.all_to_all(cot_rows.reshape(local_count, groups, capacity, latent_wid...  7.48 us
  transfers between devices with their start and end apart: 6, of which 5 were waited for; matrix products, arithmetic and copies ran while one was open for 4% of the time, Pallas kernels for 0%

commit v1 on v0

--- a/solution.py
+++ b/solution.py
@@ -44,7 +44,7 @@
     )
     gate_send = gate_slot.astype(jnp.bfloat16)
     dispatch_bf = hit_slot.astype(jnp.bfloat16).reshape(slot_total, tokens_here)
-    cot_full = lax.psum(partial_cot, "hidden")
+    cot_full = jnp.sum(lax.all_gather(partial_cot, "hidden"), 0)
     cot_rows = jnp.dot(
         dispatch_bf, cot_full.astype(jnp.bfloat16), preferred_element_type=jnp.float32
     ).astype(jnp.bfloat16)

time: 313 us -> 359 us (1.15)
  waiting for transfers between devices: 117 us -> 224 us
  blocking collectives: 139 us -> 68.5 us
  other arithmetic: 2.22 us -> 9.14 us
    all_gather x0 -> x1, waiting for transfers between devices: none -> 97.2 us  [on_device(): cot_full = jnp.sum(lax.all_gather(partial_cot, 'hidden'), 0)]
    psum x1 -> x0, blocking collectives: 62 us -> none  [on_device(): cot_full = lax.psum(partial_cot, 'hidden')]
    psum x1, blocking collectives: 66.5 us -> 57.9 us  [on_device(): latent_grad, gate_grad = lax.psum((token_sums, gate_local), 'hidden')]
    reduce_sum x0 -> x1, other arithmetic: none -> 7.72 us  [on_device(): cot_full = jnp.sum(lax.all_gather(partial_cot, 'hidden'), 0)]
    all_to_all x1, waiting for transfers between devices: 13.1 us -> 17.5 us  [on_device(): lax.all_to_all(latent_back, 'expert', split_axis=1, concat_axis=1, tiled=...]
  transfers between devices with their start and end apart: 6 -> 7, of which waited for: 5 -> 6; matrix products, arithmetic and copies ran while one was open for 4% -> 3% of each run, Pallas kernels for 0% -> 0%
where the time goes in v1:
time: 359 us; the launch traced here: 358 us
  waiting for transfers between devices  224 us (62%)
  blocking collectives  68.5 us (19%)
  starting transfers between devices  22.6 us (6%)
  matrix products  17 us (5%)
  between operations  15.7 us (4%)
  other arithmetic  9.14 us (3%)
    all_gather x1, waiting for transfers between devices, on_device(): cot_full = jnp.sum(lax.all_gather(partial_cot, 'hidden'), 0)  97.2 us
    reduce_scatter x1, waiting for transfers between devices, on_device(): lax.psum_scatter(down_term, 'expert', scatter_dimension=0, tiled=True)  79.1 us
    psum x1, blocking collectives, on_device(): latent_grad, gate_grad = lax.psum((token_sums, gate_local), 'hidden')  57.9 us
    all_to_all x1, waiting for transfers between devices, on_device(): lax.all_to_all(latent_back, 'expert', split_axis=1, concat_axis=1, tiled=...  17.5 us
    all_to_all x1, waiting for transfers between devices, on_device(): lax.all_to_all(cot_rows.reshape(local_count, groups, capacity, latent_wid...  12.2 us
    all_to_all x1, waiting for transfers between devices, on_device(): lax.all_to_all(latent_rows.reshape(local_count, groups, capacity, latent_...  12 us
    all_to_all x1, blocking collectives, on_device(): lax.all_to_all(gate_send, 'expert', split_axis=1, concat_axis=1, tiled=True)  10.6 us
    reduce_sum x1, other arithmetic, on_device(): cot_full = jnp.sum(lax.all_gather(partial_cot, 'hidden'), 0)  7.72 us
  transfers between devices with their start and end apart: 7, of which 6 were waited for; matrix products, arithmetic and copies ran while one was open for 3% of the time, Pallas kernels for 0%

profile of v1, /device:TPU:2, one launch (start us, length us, event | category | flops | bytes accessed | tf_op | source)
XLA Modules:
  0.0 358.4 jit_solution(8465886604232787866)
XLA Ops:
  8.1 2.5 fusion.23
  11.8 97.2 %all-gather.3.cloned.1.call-done = f32[4096,1024]{1,0:T(8,128)} async-done(((f32[256,1024]{1,0:T(8,128)}), f32[4096,1024]{1,0:T(8,128)}) %all-gather.3.cloned.1.call-update) | async-done | bytes 16777232 | tf_op jit(solution)/shard_map/all_gather | solution.py:47
  109.0 7.7 %reduce_sum.68 = bf16[256,1024]{1,0:T(8,128)(2,1)S(1)} reduce(f32[16,256,1024]{2,1,0:T(8,128)} %bitcast.86, f32[]{:T(128)} %constant.3.clone.1), dimensions={0}, to_apply=%region_5.6 | reduce | flops 3932160 | bytes 17301508 | tf_op jit(solution)/shard_map/reduce_sum | solution.py:47
  116.8 1.3 convolution_convert_fusion
  118.0 7.3 %all-to-all-start.2 = ((bf16[1,16,24,1024]{3,2,0,1:T(8,128)(2,1)}), bf16[1,16,24,1024]{3,2,0,1:T(8,128)(2,1)S(1)}, u32[]{:S(2)}, u32[]{:S(2)}) async-start(bf16[1,16,24,1024]{3,2,0,1:T(8,128)(2,1)} %bitcast.12), calls=%async_computation.2 | async-start | bytes 1572864 | tf_op jit(solution)/shard_map/all_to_all | solution.py:55
  125.3 1.3 convolution_convert_fusion.1
  126.6 12.2 %all-to-all-done.2 = bf16[1,16,24,1024]{3,2,0,1:T(8,128)(2,1)S(1)} async-done(((bf16[1,16,24,1024]{3,2,0,1:T(8,128)(2,1)}), bf16[1,16,24,1024]{3,2,0,1:T(8,128)(2,1)S(1)}, u32[]{:S(2)}, u32[]{:S(2)}) %all-to-all-start.2) | async-done | bytes 786464 | tf_op jit(solution)/shard_map/all_to_all | solution.py:55
  138.7 4.8 %all-to-all-start.1 = ((bf16[1,16,24,1024]{3,2,0,1:T(8,128)(2,1)}), bf16[1,16,24,1024]{3,2,0,1:T(8,128)(2,1)S(1)}, u32[]{:S(2)}, u32[]{:S(2)}) async-start(bf16[1,16,24,1024]{3,2,0,1:T(8,128)(2,1)} %bitcast.7), calls=%async_computation.1 | async-start | bytes 1572864 | tf_op jit(solution)/shard_map/all_to_all | solution.py:62
  144.0 12.0 %all-to-all-done.1 = bf16[1,16,24,1024]{3,2,0,1:T(8,128)(2,1)S(1)} async-done(((bf16[1,16,24,1024]{3,2,0,1:T(8,128)(2,1)}), bf16[1,16,24,1024]{3,2,0,1:T(8,128)(2,1)S(1)}, u32[]{:S(2)}, u32[]{:S(2)}) %all-to-all-start.1) | async-done | bytes 786464 | tf_op jit(solution)/shard_map/all_to_all | solution.py:62
  156.5 0.7 reshape.184
  157.2 4.7 %all-to-all-start.4 = ((f32[1,16,24]{2,0,1:T(1,128)}), f32[1,16,24]{2,0,1:T(1,128)S(1)}, u32[]{:S(2)}, u32[]{:S(2)}) async-start(f32[1,16,24]{2,0,1:T(1,128)} %reshape.184), calls=%async_computation.6 | async-start | bytes 16384 | tf_op jit(solution)/shard_map/all_to_all | solution.py:100
  161.9 6.2 %all-to-all-done.4 = f32[1,16,24]{2,0,1:T(1,128)S(1)} async-done(((f32[1,16,24]{2,0,1:T(1,128)}), f32[1,16,24]{2,0,1:T(1,128)S(1)}, u32[]{:S(2)}, u32[]{:S(2)}) %all-to-all-start.4) | async-done | bytes 1568 | tf_op jit(solution)/shard_map/all_to_all | solution.py:100
  168.5 10.6 %all_to_all.25 = bf16[1,16,24]{2,0,1:T(2,128)(2,1)S(1)} all-to-all(bf16[1,16,24]{2,0,1:T(2,128)(2,1)S(1)} %copy.45), channel_id=1, replica_groups=mesh['expert'=16,'hidden'=16] {'expert'}, dimensions={1} | all-to-all | bytes 1536 | tf_op jit(solution)/shard_map/all_to_all | solution.py:69
  179.5 1.5 convolution_bitcast_fusion
  181.0 5.7 %all-to-all-start.3 = ((f32[1,16,24,1024]{3,2,0,1:T(8,128)}), f32[1,16,24,1024]{3,2,0,1:T(8,128)}, u32[]{:S(2)}, u32[]{:S(2)}) async-start(f32[1,16,24,1024]{3,2,0,1:T(8,128)} %convolution_bitcast_fusion), calls=%async_computation.3 | async-start | bytes 3145728 | tf_op jit(solution)/shard_map/all_to_all | solution.py:99
  186.8 1.3 fusion.24
  188.2 17.5 %all-to-all-done.3 = f32[1,16,24,1024]{3,2,0,1:T(8,128)} async-done(((f32[1,16,24,1024]{3,2,0,1:T(8,128)}), f32[1,16,24,1024]{3,2,0,1:T(8,128)}, u32[]{:S(2)}, u32[]{:S(2)}) %all-to-all-start.3) | async-done | bytes 1572896 | tf_op jit(solution)/shard_map/all_to_all | solution.py:99
  205.7 3.5 fusion.2
  209.2 57.9 %all-reduce.2 = (bf16[256,1024]{1,0:T(8,128)(2,1)S(1)}, f32[256,22]{0,1:T(8,128)}) all-reduce(f32[256,1024]{1,0:T(8,128)} %fusion.2, f32[256,22]{0,1:T(8,128)S(1)} %get-tuple-element.6), channel_id=1, replica_groups=mesh['expert'=16,'hidden'=16] {'hidden'}, use_global_device_ids=true, to_apply=%region_6.7 | all-reduce | flops 267776 | bytes 1617920 | tf_op jit(solution)/shard_map/psum | solution.py:111
  267.1 1.3 fusion.25
  268.5 1.2 convolution_bitcast_fusion.2
  269.7 1.2 convolution_bitcast_fusion.1
  270.9 1.0 convolution_convert_fusion.2
  271.8 79.1 %reduce-scatter.3.cloned.1.call-done = f32[64,256]{1,0:T(8,128)} async-done(((f32[1024,256]{1,0:T(8,128)}), f32[64,256]{1,0:T(8,128)}) %reduce-scatter.3.cloned.1.call-update) | async-done | bytes 65552 | tf_op jit(solution)/shard_map/reduce_scatter | solution.py:121
  (48 shorter events, 3.0 us)
Async XLA Ops:
  8.0 117.3 %copy-start = (bf16[256,1024]{1,0:T(8,128)(2,1)S(1)}, bf16[256,1024]{1,0:T(8,128)(2,1)}, u32[]{:S(2)}) copy-start(bf16[256,1024]{1,0:T(8,128)(2,1)} %param.12) | copy-start | bytes 1572868
  8.0 2.6 copy-start.7
  8.0 101.0 %all-gather.3.cloned.1.call-start = ((), (), s32[]{:S(2)}) async-start(), calls=%async_computation.9 | async-start | bytes 17825792 | tf_op jit(solution)/shard_map/all_gather | solution.py:47
  118.0 20.7 %all-to-all-start.2 = ((bf16[1,16,24,1024]{3,2,0,1:T(8,128)(2,1)}), bf16[1,16,24,1024]{3,2,0,1:T(8,128)(2,1)S(1)}, u32[]{:S(2)}, u32[]{:S(2)}) async-start(bf16[1,16,24,1024]{3,2,0,1:T(8,128)(2,1)} %bitcast.12), calls=%async_computation.2 | async-start | bytes 1572864 | tf_op jit(solution)/shard_map/all_to_all | solution.py:55
  125.3 18.3 %copy-start.5 = (bf16[1,168,1024]{2,1,0:T(8,128)(2,1)S(1)}, bf16[1,168,1024]{2,1,0:T(8,128)(2,1)}, u32[]{:S(2)}) copy-start(bf16[1,168,1024]{2,1,0:T(8,128)(2,1)} %param.19) | copy-start | bytes 1032196
  126.6 29.4 %copy-start.1 = (bf16[1,1024,168]{1,2,0:T(8,128)(2,1)S(1)}, bf16[1,1024,168]{1,2,0:T(8,128)(2,1)}, u32[]{:S(2)}) copy-start(bf16[1,1024,168]{1,2,0:T(8,128)(2,1)} %param.18) | copy-start | bytes 1032196
  138.7 17.3 %all-to-all-start.1 = ((bf16[1,16,24,1024]{3,2,0,1:T(8,128)(2,1)}), bf16[1,16,24,1024]{3,2,0,1:T(8,128)(2,1)S(1)}, u32[]{:S(2)}, u32[]{:S(2)}) async-start(bf16[1,16,24,1024]{3,2,0,1:T(8,128)(2,1)} %bitcast.7), calls=%async_computation.1 | async-start | bytes 1572864 | tf_op jit(solution)/shard_map/all_to_all | solution.py:62
  143.5 18.3 %copy-start.8 = (bf16[256,22]{0,1:T(8,128)(2,1)S(1)}, bf16[256,22]{0,1:T(8,128)(2,1)}, u32[]{:S(2)}) copy-start(bf16[256,22]{0,1:T(8,128)(2,1)} %param.15) | copy-start | bytes 33796
  157.2 10.9 %all-to-all-start.4 = ((f32[1,16,24]{2,0,1:T(1,128)}), f32[1,16,24]{2,0,1:T(1,128)S(1)}, u32[]{:S(2)}, u32[]{:S(2)}) async-start(f32[1,16,24]{2,0,1:T(1,128)} %reshape.184), calls=%async_computation.6 | async-start | bytes 16384 | tf_op jit(solution)/shard_map/all_to_all | solution.py:100
  181.0 5.8 %copy-start.2 = (bf16[256,1024]{1,0:T(8,128)(2,1)S(1)}, bf16[256,1024]{1,0:T(8,128)(2,1)}, u32[]{:S(2)}) copy-start(bf16[256,1024]{1,0:T(8,128)(2,1)} %param.13) | copy-start | bytes 1572868
  181.0 5.8 %copy-start.4 = (bf16[256,256]{1,0:T(8,128)(2,1)S(1)}, bf16[256,256]{1,0:T(8,128)(2,1)}, u32[]{:S(2)}) copy-start(bf16[256,256]{1,0:T(8,128)(2,1)} %param.11) | copy-start | bytes 393220
  181.0 24.7 %all-to-all-start.3 = ((f32[1,16,24,1024]{3,2,0,1:T(8,128)}), f32[1,16,24,1024]{3,2,0,1:T(8,128)}, u32[]{:S(2)}, u32[]{:S(2)}) async-start(f32[1,16,24,1024]{3,2,0,1:T(8,128)} %convolution_bitcast_fusion), calls=%async_computation.3 | async-start | bytes 3145728 | tf_op jit(solution)/shard_map/all_to_all | solution.py:99
  186.7 85.1 %reduce-scatter.5.cloned.1.call-start = ((), (), s32[]{:S(2)}) async-start(), calls=%async_computation.8 | async-start | bytes 1114112 | tf_op jit(solution)/shard_map/reduce_scatter | solution.py:122
  188.1 79.0 %copy-start.6 = (bf16[256,256]{1,0:T(8,128)(2,1)S(1)}, bf16[256,256]{1,0:T(8,128)(2,1)}, u32[]{:S(2)}) copy-start(bf16[256,256]{1,0:T(8,128)(2,1)} %param.10) | copy-start | bytes 393220
  188.1 162.8 %reduce-scatter.3.cloned.1.call-start = ((), (), s32[]{:S(2)}) async-start(), calls=%async_computation.7 | async-start | bytes 1114112 | tf_op jit(solution)/shard_map/reduce_scatter | solution.py:121
  268.5 2.4 copy-start.3
Sparse Core Ops, SparseCore 0:
  10.7 98.2 all-gather.2
Sparse Core Ops, SparseCore 1:
  191.2 77.2 reduce-scatter.4
  272.5 78.4 reduce-scatter.2
